TPU v7x, 128 devices: a whole 4x4x4 slice. The times are simulated.
128 devices in a mesh: depth: 128 (over x, z, y, core).
Axes of the slice: x: 4, y: 4, z: 4, core: 2. Of those that a mesh axis runs over, the one named last changes fastest.
Arguments:
- initial: bfloat16 [2, 256, 1536], replicated, may hold values from -6 to 6
- weights: bfloat16 [256, 1536, 1536], P('depth'), may hold values from -0.15625 to 0.15625
- biases: float32 [256, 1536], P('depth'), may hold values from -3 to 3
- step_sizes: float32 [256], P('depth'), may hold values from 0.02 to 0.2
Outputs:
- states: bfloat16 [256, 2, 256, 1536], P('depth')
All inputs are finite; a program needn't handle non-finite values.
Results may differ from a plain program's by a relative error of at most 0.013.
The roundings to bfloat16 on the way count: a program that leaves them out, or rounds other values in their place, can miss the bound.
Values may be sent and summed in bfloat16 or wider, within the bound.
A program may use at most 64 MiB of HBM per device.

v0:
```python
import jax
import jax.numpy as jnp
from jax import lax
from jax.sharding import PartitionSpec as P

LAY_DEV = 2
INTERVAL = 8


row_blocks = 8


def passed_along(value, axis, steps):
    count = lax.axis_size(axis)
    leading, last = (max(0, -steps), min(count, count - steps))
    return lax.ppermute(value, axis, [(source, source + steps) for source in range(leading, last)])


def advance(entering, weights, biases, step_sizes):
    state = entering.astype(jnp.float32)
    outputs = []
    for layer in range(LAY_DEV):
        pre = (
            jnp.dot(state.astype(jnp.bfloat16), weights[layer], preferred_element_type=jnp.float32)
            + biases[layer]
        )
        state = state + step_sizes[layer] * jnp.tanh(pre)
        outputs.append(state)
    return jnp.stack(outputs)


def local(initial, weights, biases, step_sizes):
    device = lax.axis_index("depth")
    count = lax.axis_size("depth")
    groups = count // INTERVAL
    interval_index = device // INTERVAL
    width = initial.shape[2]
    start_state = initial.reshape(-1, width)
    entering = start_state
    passes = []
    for relax_pass in range(3):
        leaving = advance(entering, weights, biases, step_sizes)[-1].astype(jnp.bfloat16)
        arrived = passed_along(leaving, "depth", 1)
        entering = jnp.where(device == 0, start_state, arrived)
        passes.append(entering)
    entry_state = passes[1]
    fresh_state = passes[2]
    anchor = entry_state.astype(jnp.float32)
    residual_local = fresh_state.astype(jnp.float32) - anchor
    residual_ahead = passed_along(residual_local.astype(jnp.bfloat16), "depth", -INTERVAL).astype(
        residual_local.dtype
    )
    coarse_step = INTERVAL * LAY_DEV * step_sizes[0]

    def coarse_update(correction, base, residual):
        rows_here = base.shape[0]
        stacked = jnp.concatenate([base + correction.astype(jnp.float32), base], axis=0)
        pre = (
            jnp.dot(stacked.astype(jnp.bfloat16), weights[0], preferred_element_type=jnp.float32)
            + biases[0]
        )
        mapped = stacked + coarse_step * jnp.tanh(pre)
        return (mapped[:rows_here] - mapped[rows_here:] + residual).astype(jnp.bfloat16)

    def silent(correction, base, residual):
        return jnp.zeros_like(correction)

    zero_block = jnp.zeros_like(start_state)
    piece_rows = start_state.shape[0] // row_blocks

    def blocked_link(step_index, correction):
        send_block = step_index - interval_index
        sending = (send_block >= 0) & (send_block < row_blocks) & (interval_index < groups - 1)
        send_start = jnp.clip(send_block, 0, row_blocks - 1) * piece_rows
        part_correction = lax.dynamic_slice_in_dim(correction, send_start, piece_rows, 0)
        part_anchor = lax.dynamic_slice_in_dim(anchor, send_start, piece_rows, 0)
        part_residual = lax.dynamic_slice_in_dim(residual_ahead, send_start, piece_rows, 0)
        message = lax.cond(
            sending, coarse_update, silent, part_correction, part_anchor, part_residual
        )
        arrived = passed_along(message, "depth", INTERVAL)
        take_block = step_index - interval_index + 1
        taking = (interval_index >= 1) & (take_block >= 0) & (take_block < row_blocks)
        take_start = jnp.clip(take_block, 0, row_blocks - 1) * piece_rows
        current = lax.dynamic_slice_in_dim(correction, take_start, piece_rows, 0)
        updated = jnp.where(taking, arrived, current)
        return lax.dynamic_update_slice_in_dim(correction, updated, take_start, 0)

    correction = lax.fori_loop(0, groups - 2 + row_blocks, blocked_link, zero_block)
    corrected = anchor + correction.astype(jnp.float32)
    states = advance(corrected, weights, biases, step_sizes).astype(jnp.bfloat16)
    return states.reshape(states.shape[0], 2, -1, width)


def solution(mesh):
    placed = (P(), P("depth", None, None), P("depth", None), P("depth"))
    return jax.shard_map(
        local, mesh=mesh, in_specs=placed, out_specs=P("depth", None, None, None), check_vma=False
    )
```

profile of v0, /device:TPU:102, one launch (start us, length us, event | category | flops | bytes accessed | tf_op | source)
XLA Modules:
  0.0 463.7 jit_solution(11905397995412473867)
XLA Ops:
  2.2 6.8 %fusion.45 = f32[512,1536]{1,0:T(8,128)S(1)} fusion(bf16[512,1536]{1,0:T(8,128)(2,1)} %bitcast.114, bf16[2,1536,1536]{2,1,0:T(8,128)(2,1)} %param.9, f32[1536]{0:T(1024)S(1)} %get-tuple-element.294, f32[]{:T(128)} %bitcast.2), kind=kOutput, calls=%fused_computation.36 | convolution fusion | flops 2419064832 | bytes 11016704 | tf_op jit(solution)/shard_map/dot_general | solution.py:24
  9.1 3.5 fusion.148
  14.6 22.0 %collective-permute-done.1 = bf16[512,1536]{1,0:T(8,128)(2,1)} collective-permute-done((bf16[512,1536]{1,0:T(8,128)(2,1)S(1)}, bf16[512,1536]{1,0:T(8,128)(2,1)}, u32[]{:S(2)}, u32[]{:S(2)}) %collective-permute-start.1) | collective-permute-done | bytes 1572896 | tf_op jit(solution)/shard_map/ppermute | solution.py:16
  36.6 7.2 %convert_add_fusion.2 = f32[512,1536]{1,0:T(8,128)S(1)} fusion(bf16[2,1536,1536]{2,1,0:T(8,128)(2,1)} %param.9, bf16[512,1536]{1,0:T(8,128)(2,1)S(1)} %bitcast.115, bf16[512,1536]{1,0:T(8,128)(2,1)} %collective-permute-done.1, f32[1536]{0:T(1024)S(1)} %get-tuple-element.294, f32[]{:T(128)} %bitcast.2, pred[]{:T(512)S(6)} %eq.2), kind=kOutput, calls=%fused_computation.67 | convolution fusion | flops 2420637696 | bytes 14165504 | tf_op jit(solution)/shard_map/dot_general | solution.py:24
  43.8 5.8 %fusion.145 = bf16[512,1536]{1,0:T(8,128)(2,1)S(1)} fusion(f32[512,1536]{1,0:T(8,128)S(1)} %convert_add_fusion.2, bf16[2,1536,1536]{2,1,0:T(8,128)(2,1)} %param.9, f32[1536]{0:T(1024)S(1)} %get-tuple-element.293, f32[]{:T(128)} %bitcast.4), kind=kOutput, calls=%fused_computation.78 | convolution fusion | flops 2419851264 | bytes 12591616 | tf_op jit(solution)/shard_map/dot_general | solution.py:24
  51.5 21.9 %collective-permute-done.2 = bf16[512,1536]{1,0:T(8,128)(2,1)S(1)} collective-permute-done((bf16[512,1536]{1,0:T(8,128)(2,1)S(1)}, bf16[512,1536]{1,0:T(8,128)(2,1)S(1)}, u32[]{:S(2)}, u32[]{:S(2)}) %collective-permute-start.2) | collective-permute-done | bytes 1572896 | tf_op jit(solution)/shard_map/ppermute | solution.py:16
  84.4 21.7 %collective-permute-done.3 = bf16[512,1536]{1,0:T(8,128)(2,1)S(1)} collective-permute-done((bf16[512,1536]{1,0:T(8,128)(2,1)S(1)}, bf16[512,1536]{1,0:T(8,128)(2,1)S(1)}, u32[]{:S(2)}, u32[]{:S(2)}) %collective-permute-start.3) | collective-permute-done | bytes 1572896 | tf_op jit(solution)/shard_map/ppermute | solution.py:16
  110.9 24.9 %collective-permute-done.4 = bf16[512,1536]{1,0:T(8,128)(2,1)} collective-permute-done((bf16[512,1536]{1,0:T(8,128)(2,1)S(1)}, bf16[512,1536]{1,0:T(8,128)(2,1)}, u32[]{:S(2)}, u32[]{:S(2)}) %collective-permute-start.4) | collective-permute-done | bytes 1572896 | tf_op jit(solution)/shard_map/ppermute | solution.py:16
  138.9 311.5 %while.14 = (s32[]{:T(128)}, bf16[512,1536]{1,0:T(8,128)(2,1)}, s32[]{:T(128)}, pred[]{:T(512)}, pred[]{:T(512)}, /*index=5*/f32[512,1536]{1,0:T(8,128)}, f32[]{...) while((s32[]{:T(128)}, bf16[512,1536]{1,0:T(8,128)(2,1)}, ...), condition=%wide.region_3.4_spmd, body=%wide.region_0.3_spmd.sunk | while | flops 605749248 | bytes 11228131 | solution.py:89
  140.2 8.4 %collective-permute-done = bf16[64,1536]{1,0:T(8,128)(2,1)S(1)} collective-permute-done((bf16[64,1536]{1,0:T(8,128)(2,1)S(1)}, bf16[64,1536]{1,0:T(8,128)(2,1)S(1)}, u32[]{:S(2)}, u32[]{:S(2)}) %collective-permute-start) | collective-permute-done | bytes 196640 | tf_op jit(solution)/shard_map/while/body/eval_jaxpr/ppermute | solution.py:16
  151.6 6.9 %collective-permute-done = bf16[64,1536]{1,0:T(8,128)(2,1)S(1)} collective-permute-done((bf16[64,1536]{1,0:T(8,128)(2,1)S(1)}, bf16[64,1536]{1,0:T(8,128)(2,1)S(1)}, u32[]{:S(2)}, u32[]{:S(2)}) %collective-permute-start) | collective-permute-done | bytes 196640 | tf_op jit(solution)/shard_map/while/body/eval_jaxpr/ppermute | solution.py:16
  161.6 6.2 %collective-permute-done = bf16[64,1536]{1,0:T(8,128)(2,1)S(1)} collective-permute-done((bf16[64,1536]{1,0:T(8,128)(2,1)S(1)}, bf16[64,1536]{1,0:T(8,128)(2,1)S(1)}, u32[]{:S(2)}, u32[]{:S(2)}) %collective-permute-start) | collective-permute-done | bytes 196640 | tf_op jit(solution)/shard_map/while/body/eval_jaxpr/ppermute | solution.py:16
  170.8 7.0 %collective-permute-done = bf16[64,1536]{1,0:T(8,128)(2,1)S(1)} collective-permute-done((bf16[64,1536]{1,0:T(8,128)(2,1)S(1)}, bf16[64,1536]{1,0:T(8,128)(2,1)S(1)}, u32[]{:S(2)}, u32[]{:S(2)}) %collective-permute-start) | collective-permute-done | bytes 196640 | tf_op jit(solution)/shard_map/while/body/eval_jaxpr/ppermute | solution.py:16
  180.9 7.8 %collective-permute-done = bf16[64,1536]{1,0:T(8,128)(2,1)S(1)} collective-permute-done((bf16[64,1536]{1,0:T(8,128)(2,1)S(1)}, bf16[64,1536]{1,0:T(8,128)(2,1)S(1)}, u32[]{:S(2)}, u32[]{:S(2)}) %collective-permute-start) | collective-permute-done | bytes 196640 | tf_op jit(solution)/shard_map/while/body/eval_jaxpr/ppermute | solution.py:16
  191.7 8.4 %collective-permute-done = bf16[64,1536]{1,0:T(8,128)(2,1)S(1)} collective-permute-done((bf16[64,1536]{1,0:T(8,128)(2,1)S(1)}, bf16[64,1536]{1,0:T(8,128)(2,1)S(1)}, u32[]{:S(2)}, u32[]{:S(2)}) %collective-permute-start) | collective-permute-done | bytes 196640 | tf_op jit(solution)/shard_map/while/body/eval_jaxpr/ppermute | solution.py:16
  203.1 8.4 %collective-permute-done = bf16[64,1536]{1,0:T(8,128)(2,1)S(1)} collective-permute-done((bf16[64,1536]{1,0:T(8,128)(2,1)S(1)}, bf16[64,1536]{1,0:T(8,128)(2,1)S(1)}, u32[]{:S(2)}, u32[]{:S(2)}) %collective-permute-start) | collective-permute-done | bytes 196640 | tf_op jit(solution)/shard_map/while/body/eval_jaxpr/ppermute | solution.py:16
  214.5 8.4 %collective-permute-done = bf16[64,1536]{1,0:T(8,128)(2,1)S(1)} collective-permute-done((bf16[64,1536]{1,0:T(8,128)(2,1)S(1)}, bf16[64,1536]{1,0:T(8,128)(2,1)S(1)}, u32[]{:S(2)}, u32[]{:S(2)}) %collective-permute-start) | collective-permute-done | bytes 196640 | tf_op jit(solution)/shard_map/while/body/eval_jaxpr/ppermute | solution.py:16
  225.8 8.7 %collective-permute-done = bf16[64,1536]{1,0:T(8,128)(2,1)S(1)} collective-permute-done((bf16[64,1536]{1,0:T(8,128)(2,1)S(1)}, bf16[64,1536]{1,0:T(8,128)(2,1)S(1)}, u32[]{:S(2)}, u32[]{:S(2)}) %collective-permute-start) | collective-permute-done | bytes 196640 | tf_op jit(solution)/shard_map/while/body/eval_jaxpr/ppermute | solution.py:16
  237.6 10.2 %collective-permute-done = bf16[64,1536]{1,0:T(8,128)(2,1)S(1)} collective-permute-done((bf16[64,1536]{1,0:T(8,128)(2,1)S(1)}, bf16[64,1536]{1,0:T(8,128)(2,1)S(1)}, u32[]{:S(2)}, u32[]{:S(2)}) %collective-permute-start) | collective-permute-done | bytes 196640 | tf_op jit(solution)/shard_map/while/body/eval_jaxpr/ppermute | solution.py:16
  250.7 10.5 %collective-permute-done = bf16[64,1536]{1,0:T(8,128)(2,1)S(1)} collective-permute-done((bf16[64,1536]{1,0:T(8,128)(2,1)S(1)}, bf16[64,1536]{1,0:T(8,128)(2,1)S(1)}, u32[]{:S(2)}, u32[]{:S(2)}) %collective-permute-start) | collective-permute-done | bytes 196640 | tf_op jit(solution)/shard_map/while/body/eval_jaxpr/ppermute | solution.py:16
  264.3 9.9 %collective-permute-done = bf16[64,1536]{1,0:T(8,128)(2,1)S(1)} collective-permute-done((bf16[64,1536]{1,0:T(8,128)(2,1)S(1)}, bf16[64,1536]{1,0:T(8,128)(2,1)S(1)}, u32[]{:S(2)}, u32[]{:S(2)}) %collective-permute-start) | collective-permute-done | bytes 196640 | tf_op jit(solution)/shard_map/while/body/eval_jaxpr/ppermute | solution.py:16
  277.2 6.2 %collective-permute-done = bf16[64,1536]{1,0:T(8,128)(2,1)S(1)} collective-permute-done((bf16[64,1536]{1,0:T(8,128)(2,1)S(1)}, bf16[64,1536]{1,0:T(8,128)(2,1)S(1)}, u32[]{:S(2)}, u32[]{:S(2)}) %collective-permute-start) | collective-permute-done | bytes 196640 | tf_op jit(solution)/shard_map/while/body/eval_jaxpr/ppermute | solution.py:16
  286.4 6.2 %collective-permute-done = bf16[64,1536]{1,0:T(8,128)(2,1)S(1)} collective-permute-done((bf16[64,1536]{1,0:T(8,128)(2,1)S(1)}, bf16[64,1536]{1,0:T(8,128)(2,1)S(1)}, u32[]{:S(2)}, u32[]{:S(2)}) %collective-permute-start) | collective-permute-done | bytes 196640 | tf_op jit(solution)/shard_map/while/body/eval_jaxpr/ppermute | solution.py:16
  295.7 39.8 %collective-permute-done = bf16[64,1536]{1,0:T(8,128)(2,1)S(1)} collective-permute-done((bf16[64,1536]{1,0:T(8,128)(2,1)S(1)}, bf16[64,1536]{1,0:T(8,128)(2,1)S(1)}, u32[]{:S(2)}, u32[]{:S(2)}) %collective-permute-start) | collective-permute-done | bytes 196640 | tf_op jit(solution)/shard_map/while/body/eval_jaxpr/ppermute | solution.py:16
  338.5 13.3 %collective-permute-done = bf16[64,1536]{1,0:T(8,128)(2,1)S(1)} collective-permute-done((bf16[64,1536]{1,0:T(8,128)(2,1)S(1)}, bf16[64,1536]{1,0:T(8,128)(2,1)S(1)}, u32[]{:S(2)}, u32[]{:S(2)}) %collective-permute-start) | collective-permute-done | bytes 196640 | tf_op jit(solution)/shard_map/while/body/eval_jaxpr/ppermute | solution.py:16
  354.8 12.8 %collective-permute-done = bf16[64,1536]{1,0:T(8,128)(2,1)S(1)} collective-permute-done((bf16[64,1536]{1,0:T(8,128)(2,1)S(1)}, bf16[64,1536]{1,0:T(8,128)(2,1)S(1)}, u32[]{:S(2)}, u32[]{:S(2)}) %collective-permute-start) | collective-permute-done | bytes 196640 | tf_op jit(solution)/shard_map/while/body/eval_jaxpr/ppermute | solution.py:16
  370.6 12.8 %collective-permute-done = bf16[64,1536]{1,0:T(8,128)(2,1)S(1)} collective-permute-done((bf16[64,1536]{1,0:T(8,128)(2,1)S(1)}, bf16[64,1536]{1,0:T(8,128)(2,1)S(1)}, u32[]{:S(2)}, u32[]{:S(2)}) %collective-permute-start) | collective-permute-done | bytes 196640 | tf_op jit(solution)/shard_map/while/body/eval_jaxpr/ppermute | solution.py:16
  386.4 12.9 %collective-permute-done = bf16[64,1536]{1,0:T(8,128)(2,1)S(1)} collective-permute-done((bf16[64,1536]{1,0:T(8,128)(2,1)S(1)}, bf16[64,1536]{1,0:T(8,128)(2,1)S(1)}, u32[]{:S(2)}, u32[]{:S(2)}) %collective-permute-start) | collective-permute-done | bytes 196640 | tf_op jit(solution)/shard_map/while/body/eval_jaxpr/ppermute | solution.py:16
  402.3 12.8 %collective-permute-done = bf16[64,1536]{1,0:T(8,128)(2,1)S(1)} collective-permute-done((bf16[64,1536]{1,0:T(8,128)(2,1)S(1)}, bf16[64,1536]{1,0:T(8,128)(2,1)S(1)}, u32[]{:S(2)}, u32[]{:S(2)}) %collective-permute-start) | collective-permute-done | bytes 196640 | tf_op jit(solution)/shard_map/while/body/eval_jaxpr/ppermute | solution.py:16
  418.1 13.4 %collective-permute-done = bf16[64,1536]{1,0:T(8,128)(2,1)S(1)} collective-permute-done((bf16[64,1536]{1,0:T(8,128)(2,1)S(1)}, bf16[64,1536]{1,0:T(8,128)(2,1)S(1)}, u32[]{:S(2)}, u32[]{:S(2)}) %collective-permute-start) | collective-permute-done | bytes 196640 | tf_op jit(solution)/shard_map/while/body/eval_jaxpr/ppermute | solution.py:16
  434.5 14.2 %collective-permute-done = bf16[64,1536]{1,0:T(8,128)(2,1)S(1)} collective-permute-done((bf16[64,1536]{1,0:T(8,128)(2,1)S(1)}, bf16[64,1536]{1,0:T(8,128)(2,1)S(1)}, u32[]{:S(2)}, u32[]{:S(2)}) %collective-permute-start) | collective-permute-done | bytes 196640 | tf_op jit(solution)/shard_map/while/body/eval_jaxpr/ppermute | solution.py:16
  450.4 8.0 %fusion.160 = (bf16[512,1536]{1,0:T(8,128)(2,1)S(1)}, f32[512,1536]{1,0:T(8,128)S(1)}) fusion(f32[1536]{0:T(1024)} %copy-done.5, bf16[2,1536,1536]{2,1,0:T(8,128)(2,1)} %get-tuple-element.438, bf16[512,1536]{1,0:T(8,128)(2,1)} %get-tuple-element.292, bf16[512,1536]{1,0:T(8,128)(2,1)} %copy-done.1, f32[]{:T(128)} %bitcast.2), kind=kOutput, calls=%fused_computation.91 | convolution fusion | flops 2424569856 | bytes 15737344 | tf_op jit(solution)/shard_map/dot_general | solution.py:24
  (125 shorter events, 95.3 us)
Async XLA Ops:
  2.2 73.3 %copy-start.5 = (f32[1536]{0:T(1024)}, f32[1536]{0:T(1024)S(1)}, u32[]{:S(2)}) copy-start(f32[1536]{0:T(1024)S(1)} %get-tuple-element.294) | copy-start | bytes 18436
  2.2 76.7 %copy-start.3 = (f32[1536]{0:T(1024)}, f32[1536]{0:T(1024)S(1)}, u32[]{:S(2)}) copy-start(f32[1536]{0:T(1024)S(1)} %get-tuple-element.293) | copy-start | bytes 18436
  12.6 24.0 %collective-permute-start.1 = (bf16[512,1536]{1,0:T(8,128)(2,1)S(1)}, bf16[512,1536]{1,0:T(8,128)(2,1)}, u32[]{:S(2)}, u32[]{:S(2)}) collective-permute-start(bf16[512,1536]{1,0:T(8,128)(2,1)S(1)} %fusion.148), channel_id=1, source_target_pairs={{0,1},{1,2},{2,3},{3,4},{4,5},{5,6},{6,7},{7,8},{8,9},{9,10},{10,1... | collective-permute-start | bytes 4718600 | tf_op jit(solution)/shard_map/ppermute | solution.py:16
  36.6 39.0 %slice-start = ((s8[9437184]{0:T(1024)(128)(4,1)}), s8[4194304]{0:T(1024)(128)(4,1)S(1)}, s32[]{:S(2)}) async-start(s8[9437184]{0:T(1024)(128)(4,1)} %bitcast.118), calls=%async_computation | async-start | bytes 8388608
  36.6 39.0 %slice-start.1 = ((s8[9437184]{0:T(1024)(128)(4,1)}), s8[4194304]{0:T(1024)(128)(4,1)S(1)}, s32[]{:S(2)}) async-start(s8[9437184]{0:T(1024)(128)(4,1)} %bitcast.118), calls=%async_computation.1 | async-start | bytes 8388608
  43.8 31.8 %slice-start.2 = ((s8[9437184]{0:T(1024)(128)(4,1)}), s8[1048576]{0:T(1024)(128)(4,1)S(1)}, s32[]{:S(2)}) async-start(s8[9437184]{0:T(1024)(128)(4,1)} %bitcast.118), calls=%async_computation.2 | async-start | bytes 2097152
  49.6 23.8 %collective-permute-start.2 = (bf16[512,1536]{1,0:T(8,128)(2,1)S(1)}, bf16[512,1536]{1,0:T(8,128)(2,1)S(1)}, u32[]{:S(2)}, u32[]{:S(2)}) collective-permute-start(bf16[512,1536]{1,0:T(8,128)(2,1)S(1)} %fusion.145), channel_id=1, source_target_pairs={{0,1},{1,2},{2,3},{3,4},{4,5},{5,6},{6,7},{7,8},{8,9},{9,10},{10,1... | collective-permute-start | bytes 4718600 | tf_op jit(solution)/shard_map/ppermute | solution.py:16
  75.5 30.6 %copy-start.1 = (bf16[512,1536]{1,0:T(8,128)(2,1)}, bf16[512,1536]{1,0:T(8,128)(2,1)S(1)}, u32[]{:S(2)}) copy-start(bf16[512,1536]{1,0:T(8,128)(2,1)S(1)} %get-tuple-element.316) | copy-start | bytes 4718596
  82.3 23.8 %collective-permute-start.3 = (bf16[512,1536]{1,0:T(8,128)(2,1)S(1)}, bf16[512,1536]{1,0:T(8,128)(2,1)S(1)}, u32[]{:S(2)}, u32[]{:S(2)}) collective-permute-start(bf16[512,1536]{1,0:T(8,128)(2,1)S(1)} %fusion.142), channel_id=1, source_target_pairs={{0,1},{1,2},{2,3},{3,4},{4,5},{5,6},{6,7},{7,8},{8,9},{9,10},{10,1... | collective-permute-start | bytes 4718600 | tf_op jit(solution)/shard_map/ppermute | solution.py:16
  106.8 29.0 %collective-permute-start.4 = (bf16[512,1536]{1,0:T(8,128)(2,1)S(1)}, bf16[512,1536]{1,0:T(8,128)(2,1)}, u32[]{:S(2)}, u32[]{:S(2)}) collective-permute-start(bf16[512,1536]{1,0:T(8,128)(2,1)S(1)} %subtract_convert_fusion), channel_id=1, source_target_pairs={{8,0},{9,1},{10,2},{11,3},{12,4},{13,5},{14,6},{15,7},{16,8},{17,9... | collective-permute-start | bytes 4718600 | tf_op jit(solution)/shard_map/ppermute | solution.py:16
  138.9 9.7 %collective-permute-start = (bf16[64,1536]{1,0:T(8,128)(2,1)S(1)}, bf16[64,1536]{1,0:T(8,128)(2,1)S(1)}, u32[]{:S(2)}, u32[]{:S(2)}) collective-permute-start(bf16[64,1536]{1,0:T(8,128)(2,1)S(1)} %get-tuple-element.432), channel_id=1, source_target_pairs={{0,8},{1,9},{2,10},{3,11},{4,12},{5,13},{6,14},{7,15},{8,16},{9,17... | collective-permute-start | bytes 589832 | tf_op jit(solution)/shard_map/while/body/eval_jaxpr/ppermute | solution.py:16
  150.3 8.3 %collective-permute-start = (bf16[64,1536]{1,0:T(8,128)(2,1)S(1)}, bf16[64,1536]{1,0:T(8,128)(2,1)S(1)}, u32[]{:S(2)}, u32[]{:S(2)}) collective-permute-start(bf16[64,1536]{1,0:T(8,128)(2,1)S(1)} %get-tuple-element.432), channel_id=1, source_target_pairs={{0,8},{1,9},{2,10},{3,11},{4,12},{5,13},{6,14},{7,15},{8,16},{9,17... | collective-permute-start | bytes 589832 | tf_op jit(solution)/shard_map/while/body/eval_jaxpr/ppermute | solution.py:16
  160.2 7.6 %collective-permute-start = (bf16[64,1536]{1,0:T(8,128)(2,1)S(1)}, bf16[64,1536]{1,0:T(8,128)(2,1)S(1)}, u32[]{:S(2)}, u32[]{:S(2)}) collective-permute-start(bf16[64,1536]{1,0:T(8,128)(2,1)S(1)} %get-tuple-element.432), channel_id=1, source_target_pairs={{0,8},{1,9},{2,10},{3,11},{4,12},{5,13},{6,14},{7,15},{8,16},{9,17... | collective-permute-start | bytes 589832 | tf_op jit(solution)/shard_map/while/body/eval_jaxpr/ppermute | solution.py:16
  169.5 8.3 %collective-permute-start = (bf16[64,1536]{1,0:T(8,128)(2,1)S(1)}, bf16[64,1536]{1,0:T(8,128)(2,1)S(1)}, u32[]{:S(2)}, u32[]{:S(2)}) collective-permute-start(bf16[64,1536]{1,0:T(8,128)(2,1)S(1)} %get-tuple-element.432), channel_id=1, source_target_pairs={{0,8},{1,9},{2,10},{3,11},{4,12},{5,13},{6,14},{7,15},{8,16},{9,17... | collective-permute-start | bytes 589832 | tf_op jit(solution)/shard_map/while/body/eval_jaxpr/ppermute | solution.py:16
  179.5 9.2 %collective-permute-start = (bf16[64,1536]{1,0:T(8,128)(2,1)S(1)}, bf16[64,1536]{1,0:T(8,128)(2,1)S(1)}, u32[]{:S(2)}, u32[]{:S(2)}) collective-permute-start(bf16[64,1536]{1,0:T(8,128)(2,1)S(1)} %get-tuple-element.432), channel_id=1, source_target_pairs={{0,8},{1,9},{2,10},{3,11},{4,12},{5,13},{6,14},{7,15},{8,16},{9,17... | collective-permute-start | bytes 589832 | tf_op jit(solution)/shard_map/while/body/eval_jaxpr/ppermute | solution.py:16
  190.4 9.7 %collective-permute-start = (bf16[64,1536]{1,0:T(8,128)(2,1)S(1)}, bf16[64,1536]{1,0:T(8,128)(2,1)S(1)}, u32[]{:S(2)}, u32[]{:S(2)}) collective-permute-start(bf16[64,1536]{1,0:T(8,128)(2,1)S(1)} %get-tuple-element.432), channel_id=1, source_target_pairs={{0,8},{1,9},{2,10},{3,11},{4,12},{5,13},{6,14},{7,15},{8,16},{9,17... | collective-permute-start | bytes 589832 | tf_op jit(solution)/shard_map/while/body/eval_jaxpr/ppermute | solution.py:16
  201.8 9.7 %collective-permute-start = (bf16[64,1536]{1,0:T(8,128)(2,1)S(1)}, bf16[64,1536]{1,0:T(8,128)(2,1)S(1)}, u32[]{:S(2)}, u32[]{:S(2)}) collective-permute-start(bf16[64,1536]{1,0:T(8,128)(2,1)S(1)} %get-tuple-element.432), channel_id=1, source_target_pairs={{0,8},{1,9},{2,10},{3,11},{4,12},{5,13},{6,14},{7,15},{8,16},{9,17... | collective-permute-start | bytes 589832 | tf_op jit(solution)/shard_map/while/body/eval_jaxpr/ppermute | solution.py:16
  213.1 9.7 %collective-permute-start = (bf16[64,1536]{1,0:T(8,128)(2,1)S(1)}, bf16[64,1536]{1,0:T(8,128)(2,1)S(1)}, u32[]{:S(2)}, u32[]{:S(2)}) collective-permute-start(bf16[64,1536]{1,0:T(8,128)(2,1)S(1)} %get-tuple-element.432), channel_id=1, source_target_pairs={{0,8},{1,9},{2,10},{3,11},{4,12},{5,13},{6,14},{7,15},{8,16},{9,17... | collective-permute-start | bytes 589832 | tf_op jit(solution)/shard_map/while/body/eval_jaxpr/ppermute | solution.py:16
  224.5 10.0 %collective-permute-start = (bf16[64,1536]{1,0:T(8,128)(2,1)S(1)}, bf16[64,1536]{1,0:T(8,128)(2,1)S(1)}, u32[]{:S(2)}, u32[]{:S(2)}) collective-permute-start(bf16[64,1536]{1,0:T(8,128)(2,1)S(1)} %get-tuple-element.432), channel_id=1, source_target_pairs={{0,8},{1,9},{2,10},{3,11},{4,12},{5,13},{6,14},{7,15},{8,16},{9,17... | collective-permute-start | bytes 589832 | tf_op jit(solution)/shard_map/while/body/eval_jaxpr/ppermute | solution.py:16
  236.2 11.5 %collective-permute-start = (bf16[64,1536]{1,0:T(8,128)(2,1)S(1)}, bf16[64,1536]{1,0:T(8,128)(2,1)S(1)}, u32[]{:S(2)}, u32[]{:S(2)}) collective-permute-start(bf16[64,1536]{1,0:T(8,128)(2,1)S(1)} %get-tuple-element.432), channel_id=1, source_target_pairs={{0,8},{1,9},{2,10},{3,11},{4,12},{5,13},{6,14},{7,15},{8,16},{9,17... | collective-permute-start | bytes 589832 | tf_op jit(solution)/shard_map/while/body/eval_jaxpr/ppermute | solution.py:16
  249.4 11.8 %collective-permute-start = (bf16[64,1536]{1,0:T(8,128)(2,1)S(1)}, bf16[64,1536]{1,0:T(8,128)(2,1)S(1)}, u32[]{:S(2)}, u32[]{:S(2)}) collective-permute-start(bf16[64,1536]{1,0:T(8,128)(2,1)S(1)} %get-tuple-element.432), channel_id=1, source_target_pairs={{0,8},{1,9},{2,10},{3,11},{4,12},{5,13},{6,14},{7,15},{8,16},{9,17... | collective-permute-start | bytes 589832 | tf_op jit(solution)/shard_map/while/body/eval_jaxpr/ppermute | solution.py:16
  263.0 11.2 %collective-permute-start = (bf16[64,1536]{1,0:T(8,128)(2,1)S(1)}, bf16[64,1536]{1,0:T(8,128)(2,1)S(1)}, u32[]{:S(2)}, u32[]{:S(2)}) collective-permute-start(bf16[64,1536]{1,0:T(8,128)(2,1)S(1)} %get-tuple-element.432), channel_id=1, source_target_pairs={{0,8},{1,9},{2,10},{3,11},{4,12},{5,13},{6,14},{7,15},{8,16},{9,17... | collective-permute-start | bytes 589832 | tf_op jit(solution)/shard_map/while/body/eval_jaxpr/ppermute | solution.py:16
  275.8 7.6 %collective-permute-start = (bf16[64,1536]{1,0:T(8,128)(2,1)S(1)}, bf16[64,1536]{1,0:T(8,128)(2,1)S(1)}, u32[]{:S(2)}, u32[]{:S(2)}) collective-permute-start(bf16[64,1536]{1,0:T(8,128)(2,1)S(1)} %get-tuple-element.432), channel_id=1, source_target_pairs={{0,8},{1,9},{2,10},{3,11},{4,12},{5,13},{6,14},{7,15},{8,16},{9,17... | collective-permute-start | bytes 589832 | tf_op jit(solution)/shard_map/while/body/eval_jaxpr/ppermute | solution.py:16
  285.1 7.6 %collective-permute-start = (bf16[64,1536]{1,0:T(8,128)(2,1)S(1)}, bf16[64,1536]{1,0:T(8,128)(2,1)S(1)}, u32[]{:S(2)}, u32[]{:S(2)}) collective-permute-start(bf16[64,1536]{1,0:T(8,128)(2,1)S(1)} %get-tuple-element.432), channel_id=1, source_target_pairs={{0,8},{1,9},{2,10},{3,11},{4,12},{5,13},{6,14},{7,15},{8,16},{9,17... | collective-permute-start | bytes 589832 | tf_op jit(solution)/shard_map/while/body/eval_jaxpr/ppermute | solution.py:16
  294.4 41.2 %collective-permute-start = (bf16[64,1536]{1,0:T(8,128)(2,1)S(1)}, bf16[64,1536]{1,0:T(8,128)(2,1)S(1)}, u32[]{:S(2)}, u32[]{:S(2)}) collective-permute-start(bf16[64,1536]{1,0:T(8,128)(2,1)S(1)} %get-tuple-element.432), channel_id=1, source_target_pairs={{0,8},{1,9},{2,10},{3,11},{4,12},{5,13},{6,14},{7,15},{8,16},{9,17... | collective-permute-start | bytes 589832 | tf_op jit(solution)/shard_map/while/body/eval_jaxpr/ppermute | solution.py:16
  337.2 14.6 %collective-permute-start = (bf16[64,1536]{1,0:T(8,128)(2,1)S(1)}, bf16[64,1536]{1,0:T(8,128)(2,1)S(1)}, u32[]{:S(2)}, u32[]{:S(2)}) collective-permute-start(bf16[64,1536]{1,0:T(8,128)(2,1)S(1)} %get-tuple-element.432), channel_id=1, source_target_pairs={{0,8},{1,9},{2,10},{3,11},{4,12},{5,13},{6,14},{7,15},{8,16},{9,17... | collective-permute-start | bytes 589832 | tf_op jit(solution)/shard_map/while/body/eval_jaxpr/ppermute | solution.py:16
  353.5 14.1 %collective-permute-start = (bf16[64,1536]{1,0:T(8,128)(2,1)S(1)}, bf16[64,1536]{1,0:T(8,128)(2,1)S(1)}, u32[]{:S(2)}, u32[]{:S(2)}) collective-permute-start(bf16[64,1536]{1,0:T(8,128)(2,1)S(1)} %get-tuple-element.432), channel_id=1, source_target_pairs={{0,8},{1,9},{2,10},{3,11},{4,12},{5,13},{6,14},{7,15},{8,16},{9,17... | collective-permute-start | bytes 589832 | tf_op jit(solution)/shard_map/while/body/eval_jaxpr/ppermute | solution.py:16
  369.3 14.1 %collective-permute-start = (bf16[64,1536]{1,0:T(8,128)(2,1)S(1)}, bf16[64,1536]{1,0:T(8,128)(2,1)S(1)}, u32[]{:S(2)}, u32[]{:S(2)}) collective-permute-start(bf16[64,1536]{1,0:T(8,128)(2,1)S(1)} %get-tuple-element.432), channel_id=1, source_target_pairs={{0,8},{1,9},{2,10},{3,11},{4,12},{5,13},{6,14},{7,15},{8,16},{9,17... | collective-permute-start | bytes 589832 | tf_op jit(solution)/shard_map/while/body/eval_jaxpr/ppermute | solution.py:16
  385.1 14.2 %collective-permute-start = (bf16[64,1536]{1,0:T(8,128)(2,1)S(1)}, bf16[64,1536]{1,0:T(8,128)(2,1)S(1)}, u32[]{:S(2)}, u32[]{:S(2)}) collective-permute-start(bf16[64,1536]{1,0:T(8,128)(2,1)S(1)} %get-tuple-element.432), channel_id=1, source_target_pairs={{0,8},{1,9},{2,10},{3,11},{4,12},{5,13},{6,14},{7,15},{8,16},{9,17... | collective-permute-start | bytes 589832 | tf_op jit(solution)/shard_map/while/body/eval_jaxpr/ppermute | solution.py:16
  401.0 14.1 %collective-permute-start = (bf16[64,1536]{1,0:T(8,128)(2,1)S(1)}, bf16[64,1536]{1,0:T(8,128)(2,1)S(1)}, u32[]{:S(2)}, u32[]{:S(2)}) collective-permute-start(bf16[64,1536]{1,0:T(8,128)(2,1)S(1)} %get-tuple-element.432), channel_id=1, source_target_pairs={{0,8},{1,9},{2,10},{3,11},{4,12},{5,13},{6,14},{7,15},{8,16},{9,17... | collective-permute-start | bytes 589832 | tf_op jit(solution)/shard_map/while/body/eval_jaxpr/ppermute | solution.py:16
  416.8 14.7 %collective-permute-start = (bf16[64,1536]{1,0:T(8,128)(2,1)S(1)}, bf16[64,1536]{1,0:T(8,128)(2,1)S(1)}, u32[]{:S(2)}, u32[]{:S(2)}) collective-permute-start(bf16[64,1536]{1,0:T(8,128)(2,1)S(1)} %get-tuple-element.432), channel_id=1, source_target_pairs={{0,8},{1,9},{2,10},{3,11},{4,12},{5,13},{6,14},{7,15},{8,16},{9,17... | collective-permute-start | bytes 589832 | tf_op jit(solution)/shard_map/while/body/eval_jaxpr/ppermute | solution.py:16
  433.2 15.6 %collective-permute-start = (bf16[64,1536]{1,0:T(8,128)(2,1)S(1)}, bf16[64,1536]{1,0:T(8,128)(2,1)S(1)}, u32[]{:S(2)}, u32[]{:S(2)}) collective-permute-start(bf16[64,1536]{1,0:T(8,128)(2,1)S(1)} %get-tuple-element.432), channel_id=1, source_target_pairs={{0,8},{1,9},{2,10},{3,11},{4,12},{5,13},{6,14},{7,15},{8,16},{9,17... | collective-permute-start | bytes 589832 | tf_op jit(solution)/shard_map/while/body/eval_jaxpr/ppermute | solution.py:16
  (5 other events, 78.3 us)
where the time goes:
time: 469 us; the launch traced here: 464 us
  waiting for transfers between devices  336 us (72%)
  other arithmetic  43.2 us (9%)
  matrix products  41.3 us (9%)
  starting transfers between devices  37.8 us (8%)
    ppermute x26, waiting for transfers between devices, passed_along(): lax.ppermute(value, axis, [(source, source + steps) for source in range(l...  336 us
    dot_general x8, matrix products, advance(): jnp.dot(state.astype(jnp.bfloat16), weights[layer], preferred_element_typ...  41.3 us
    ppermute x26, starting transfers between devices, passed_along(): lax.ppermute(value, axis, [(source, source + steps) for source in range(l...  37.8 us
    dynamic_update_slice x22, other arithmetic, blocked_link(): return lax.dynamic_update_slice_in_dim(correction, updated, take_start, 0)  36.7 us
  transfers between devices with their start and end apart: 26, of which 26 were waited for; matrix products, arithmetic and copies ran while one was open for 0% of the time, Pallas kernels for 0%

commit v1 on v0

v1 whole, which is shorter than its diff:
```python
import functools
import jax
import jax.numpy as jnp
from jax import lax
from jax.experimental import pallas as pl
from jax.experimental.pallas import tpu as pltpu
from jax.sharding import PartitionSpec as P

LAY_DEV = 2
INTERVAL = 8
MESH = pl.DeviceIdType.MESH
F32 = jnp.float32
BF16 = jnp.bfloat16

A_ROWS = 128
N_CHUNK = 3
PASS_COLS = 256
CHAIN_ROWS = (64, 64, 32, 16)
FIRST_MSG = (0, 2, 4, 8)
N_MSG = 16


def kernel(rows, width, start_hbm, w_hbm, b_ref, s_ref, out_hbm,
           w, inbuf, inbox, xout, msgout, tbuf, ubuf, xbuf, states,
           w_sem, start_sem, out_sem, x_send, x_recv, r_send, r_recv, m_send, m_recv):
    n_blocks = rows // A_ROWS
    p = lax.axis_index("depth")
    count = lax.axis_size("depth")
    groups = count // INTERVAL
    group = p // INTERVAL
    is_first = p == 0
    has_next = p < count - 1
    sends_msg = (group >= 1) & (group < groups - 1)
    res_direct = (p + 1 >= INTERVAL) & (p + 1 < 2 * INTERVAL)
    res_back = (p + 1 >= 2 * INTERVAL) & has_next
    res_target = jnp.where(res_direct, p + 1, p + 1 - INTERVAL)
    res_slot = jnp.where(res_direct, 0, 1)
    chunk = width // N_CHUNK

    load_start = pltpu.make_async_copy(start_hbm, inbuf.at[0], start_sem)
    load_start.start()
    load_w = [pltpu.make_async_copy(w_hbm.at[l], w.at[l], w_sem.at[l]) for l in range(LAY_DEV)]
    for c in load_w:
        c.start()

    barrier = pltpu.get_barrier_semaphore()
    peers = 0
    for off in (1, -1, INTERVAL, -INTERVAL, INTERVAL - 1, 1 - INTERVAL):
        ok = (p + off >= 0) & (p + off < count)
        peers = peers + jnp.where(ok, 1, 0)

        @pl.when(ok)
        def _():
            pl.semaphore_signal(barrier, inc=1, device_id=(p + off,), device_id_type=MESH)
    pl.semaphore_wait(barrier, peers)

    @pl.when(group == 0)
    def _():
        def zero(i, _):
            r = pl.multiple_of(i * 16, 16)
            inbox[0, pl.ds(r, 16), :] = jnp.zeros((16, width), BF16)
            return 0
        lax.fori_loop(0, rows // 16, zero, 0)

    def x_copy(k, b):
        r = pl.multiple_of(b * A_ROWS, A_ROWS)
        return pltpu.make_async_remote_copy(
            src_ref=xout.at[k, pl.ds(r, A_ROWS)], dst_ref=inbuf.at[k + 1, pl.ds(r, A_ROWS)],
            send_sem=x_send.at[k, b], recv_sem=x_recv.at[k, b],
            device_id=(p + 1,), device_id_type=MESH)

    def res_copy(m, r, size):
        r = pl.multiple_of(r, size)
        return pltpu.make_async_remote_copy(
            src_ref=xout.at[2, pl.ds(r, size)], dst_ref=inbox.at[res_slot, pl.ds(r, size)],
            send_sem=r_send.at[m], recv_sem=r_recv.at[res_slot, m],
            device_id=(res_target,), device_id_type=MESH)

    def res_wait(slot, m, r, size):
        r = pl.multiple_of(r, size)
        pltpu.make_async_remote_copy(
            src_ref=xout.at[2, pl.ds(r, size)], dst_ref=inbox.at[slot, pl.ds(r, size)],
            send_sem=r_send.at[m], recv_sem=r_recv.at[slot, m],
            device_id=(res_target,), device_id_type=MESH).wait_recv()

    def msg_copy(m, r, size, c):
        r = pl.multiple_of(r, size)
        cols = slice(c * chunk, (c + 1) * chunk)
        return pltpu.make_async_remote_copy(
            src_ref=msgout.at[pl.ds(r, size), cols], dst_ref=inbox.at[0, pl.ds(r, size), cols],
            send_sem=m_send.at[m, c], recv_sem=m_recv.at[m, c],
            device_id=(p + INTERVAL,), device_id_type=MESH)

    def messages(b, body):
        for i, size in enumerate(CHAIN_ROWS):
            if i and CHAIN_ROWS[i - 1] == size:
                continue
            same = [j for j in range(len(CHAIN_ROWS)) if CHAIN_ROWS[j] == size]
            per = A_ROWS // size

            @pl.when((b >= same[0]) & (b <= same[-1]))
            def _():
                def one(j, _):
                    body(FIRST_MSG[same[0]] + (b - same[0]) * per + j, b * A_ROWS + j * size, size)
                    return 0
                lax.fori_loop(0, per, one, 0)

    def relax(k, b, first):
        source = jnp.where(is_first, 0, k)
        rb = pl.multiple_of(b * A_ROWS, A_ROWS)
        rs = pl.ds(rb, A_ROWS)

        @pl.when((k > 0) & jnp.logical_not(is_first))
        def _():
            x_copy(k - 1, b).wait_recv()
        x = inbuf[source, rs, :]
        step0 = s_ref[0]
        for c in range(width // PASS_COLS):
            cols = slice(c * PASS_COLS, (c + 1) * PASS_COLS)
            pre = jnp.dot(x, w[0, :, cols], preferred_element_type=F32) + b_ref[0:1, cols]
            t = jnp.tanh(pre)
            tbuf[rs, cols] = t
            u = x[:, cols].astype(F32) + step0 * t
            ubuf[:, cols] = u
            xbuf[:, cols] = u.astype(BF16)

        @pl.when(first)
        def _():
            load_w[1].wait()
        x1 = xbuf[...]
        step1 = s_ref[1]
        for c in range(width // PASS_COLS):
            cols = slice(c * PASS_COLS, (c + 1) * PASS_COLS)
            pre = jnp.dot(x1, w[1, :, cols], preferred_element_type=F32) + b_ref[1:2, cols]
            u = ubuf[:, cols] + step1 * jnp.tanh(pre)
            xout[k, rs, cols] = u.astype(BF16)

        @pl.when((k < 2) & has_next)
        def _():
            x_copy(k, b).start()

        @pl.when((k == 2) & (res_direct | res_back))
        def _():
            def diff(j, _):
                r = pl.ds(pl.multiple_of(rb + j * 16, 16), 16)
                xout[2, r, :] = (xout[2, r, :].astype(F32) - xout[1, r, :].astype(F32)).astype(BF16)
                return 0
            lax.fori_loop(0, A_ROWS // 16, diff, 0)
            messages(b, lambda m, r, size: res_copy(m, r, size).start())

    def chain(b):
        coarse = (INTERVAL * LAY_DEV) * s_ref[0]
        anchor = jnp.where(is_first, 0, 2)

        def one(m, r0, size):
            r = pl.ds(pl.multiple_of(r0, size), size)

            @pl.when(group == 1)
            def _():
                res_wait(0, m, r0, size)

            @pl.when(group > 1)
            def _():
                for c in range(N_CHUNK):
                    msg_copy(m, r0, size, c).wait_recv()

            @pl.when(sends_msg)
            def _():
                res_wait(1, m, r0, size)
            corr = inbox[0, r, :].astype(F32)
            x = (inbuf[anchor, r, :].astype(F32) + corr).astype(BF16)
            for c in range(N_CHUNK):
                cols = slice(c * chunk, (c + 1) * chunk)
                pre = jnp.dot(x, w[0, :, cols], preferred_element_type=F32) + b_ref[0:1, cols]
                t = jnp.tanh(pre)
                d = inbox[0, r, cols].astype(F32) + coarse * (t - tbuf[r, cols])
                msgout[r, cols] = (d + inbox[1, r, cols].astype(F32)).astype(BF16)
                tbuf[r, cols] = t

                @pl.when(sends_msg)
                def _():
                    msg_copy(m, r0, size, c).start()
        messages(b, one)

    def out_copy(l, b):
        r = pl.ds(pl.multiple_of(b * A_ROWS, A_ROWS), A_ROWS)
        return pltpu.make_async_copy(states.at[l, r], out_hbm.at[l, r], out_sem.at[l, b])

    def finish(b):
        anchor = jnp.where(is_first, 0, 2)
        r = pl.ds(pl.multiple_of(b * A_ROWS, A_ROWS), A_ROWS)
        step0 = s_ref[0]
        step1 = s_ref[1]
        for c in range(width // PASS_COLS):
            cols = slice(c * PASS_COLS, (c + 1) * PASS_COLS)
            u = (inbuf[anchor, r, cols].astype(F32) + inbox[0, r, cols].astype(F32)) + step0 * tbuf[r, cols]
            ubuf[:, cols] = u
            states[0, r, cols] = u.astype(BF16)
        out_copy(0, b).start()
        x1 = states[0, r, :]
        for c in range(width // PASS_COLS):
            cols = slice(c * PASS_COLS, (c + 1) * PASS_COLS)
            pre = jnp.dot(x1, w[1, :, cols], preferred_element_type=F32) + b_ref[1:2, cols]
            u = ubuf[:, cols] + step1 * jnp.tanh(pre)
            states[1, r, cols] = u.astype(BF16)
        out_copy(1, b).start()

    load_start.wait()
    load_w[0].wait()
    lag = jnp.where(group <= 2, 1, jnp.where(group <= 5, 2, jnp.where(group <= 8, 3, 4)))

    def wave(step, _):
        def one_pass(k, _):
            b = step - k

            @pl.when((b >= 0) & (b < n_blocks))
            def _():
                relax(k, b, step == 0)
            return 0
        lax.fori_loop(0, 3, one_pass, 0)
        cb = step - 2 - lag

        @pl.when((cb >= 0) & (cb < n_blocks))
        def _():
            @pl.when(group >= 1)
            def _():
                chain(cb)
            finish(cb)
        return 0

    lax.fori_loop(0, n_blocks + 6, wave, 0)

    def drain(b, _):
        for l in range(LAY_DEV):
            out_copy(l, b).wait()

        @pl.when(has_next)
        def _():
            for k in range(2):
                x_copy(k, b).wait_send()

        @pl.when(res_direct | res_back)
        def _():
            messages(b, lambda m, r, size: res_copy(m, r, size).wait_send())

        @pl.when(sends_msg)
        def _():
            def sent(m, r, size):
                for c in range(N_CHUNK):
                    msg_copy(m, r, size, c).wait_send()
            messages(b, sent)
        return 0

    lax.fori_loop(0, n_blocks, drain, 0)


def local(initial, weights, biases, step_sizes):
    width = initial.shape[2]
    rows = initial.shape[0] * initial.shape[1]
    start = initial.reshape(rows, width)
    n_blocks = rows // A_ROWS
    dma = pltpu.SemaphoreType.DMA
    states = pl.pallas_call(
        functools.partial(kernel, rows, width),
        out_shape=jax.ShapeDtypeStruct((LAY_DEV, rows, width), BF16),
        in_specs=[
            pl.BlockSpec(memory_space=pl.ANY),
            pl.BlockSpec(memory_space=pl.ANY),
            pl.BlockSpec(memory_space=pltpu.VMEM),
            pl.BlockSpec(memory_space=pltpu.SMEM),
        ],
        out_specs=pl.BlockSpec(memory_space=pl.ANY),
        scratch_shapes=[
            pltpu.VMEM((LAY_DEV, width, width), BF16),
            pltpu.VMEM((3, rows, width), BF16),
            pltpu.VMEM((2, rows, width), BF16),
            pltpu.VMEM((3, rows, width), BF16),
            pltpu.VMEM((rows, width), BF16),
            pltpu.VMEM((rows, width), F32),
            pltpu.VMEM((A_ROWS, width), F32),
            pltpu.VMEM((A_ROWS, width), BF16),
            pltpu.VMEM((LAY_DEV, rows, width), BF16),
            dma((LAY_DEV,)),
            dma,
            dma((LAY_DEV, n_blocks)),
            dma((2, n_blocks)),
            dma((2, n_blocks)),
            dma((N_MSG,)),
            dma((2, N_MSG)),
            dma((N_MSG, N_CHUNK)),
            dma((N_MSG, N_CHUNK)),
        ],
        compiler_params=pltpu.CompilerParams(
            collective_id=0, has_side_effects=True, vmem_limit_bytes=56 * 1024 * 1024),
    )(start, weights, biases, step_sizes)
    return states.reshape(LAY_DEV, 2, -1, width)


def solution(mesh):
    placed = (P(), P("depth", None, None), P("depth", None), P("depth"))
    return jax.shard_map(
        local, mesh=mesh, in_specs=placed, out_specs=P("depth", None, None, None), check_vma=False
    )
```

time: 469 us -> 168 us (0.36); the launches traced: 464 us -> 168 us
  waiting for transfers between devices: 336 us -> 0 us
  Pallas kernels: 0 us -> 164 us
  other arithmetic: 43.2 us -> 0 us
  matrix products: 41.3 us -> 0 us
  starting transfers between devices: 37.8 us -> 0 us
    ppermute x26 -> x0, waiting for transfers between devices: 336 us -> none  [passed_along(): lax.ppermute(value, axis, [(source, source + steps) for source in range(l...]
    pallas_call x0 -> x1, Pallas kernels: none -> 164 us  [local(): pl.pallas_call(functools.partial(kernel, rows, width), out_shape=jax.Shap...]
    dot_general x8 -> x0, matrix products: 41.3 us -> none  [advance(): jnp.dot(state.astype(jnp.bfloat16), weights[layer], preferred_element_typ...]
    ppermute x26 -> x0, starting transfers between devices: 37.8 us -> none  [passed_along(): lax.ppermute(value, axis, [(source, source + steps) for source in range(l...]
    dynamic_update_slice x22 -> x0, other arithmetic: 36.7 us -> none  [blocked_link(): return lax.dynamic_update_slice_in_dim(correction, updated, take_start, 0)]
  transfers between devices with their start and end apart: 26 -> 0, of which waited for: 26 -> 0; matrix products, arithmetic and copies ran while one was open for 0% -> 0% of each run, Pallas kernels for 0% -> 0%
where the time goes in v1:
time: 168 us
  Pallas kernels  164 us (98%)
  local copies, waits for them, and re-layouts  3.76 us (2%)
    pallas_call x1, Pallas kernels, local(): pl.pallas_call(functools.partial(kernel, rows, width), out_shape=jax.Shap...  164 us
    unnamed x1, local copies, waits for them, and re-layouts  3.76 us

profile of v1, /device:TPU:102, one launch (start us, length us, event | category | flops | bytes accessed | tf_op | source)
XLA Modules:
  0.0 167.9 jit_solution(1584233217720380781)
XLA Ops:
  0.0 164.2 %shard_map.46 = bf16[2,512,1536]{2,1,0:T(8,128)(2,1)} custom-call(bf16[512,1536]{1,0:T(8,128)(2,1)} %bitcast.3, bf16[2,1536,1536]{2,1,0:T(8,128)(2,1)} %w_hbm.1, f32[2,1536]{1,0:T(2,128)} %b_ref.1, f32[2]{0:T(128)} %s_ref.1), custom_call_target="tpu_custom_call" | custom-call | tf_op jit(solution)/shard_map/pallas_call | solution.py:263
  164.2 3.8 %copy.6 = bf16[2,2,256,1536]{3,2,1,0:T(8,128)(2,1)} copy(bf16[2,2,256,1536]{3,2,1,0:T(8,128)(2,1)} %bitcast.2) | data formatting | bytes 6291456

commit v2 on v1

--- a/solution.py
+++ b/solution.py
@@ -13,11 +13,11 @@
 BF16 = jnp.bfloat16
 
 A_ROWS = 128
-N_CHUNK = 3
+N_CHUNK = 1
 PASS_COLS = 256
-CHAIN_ROWS = (64, 64, 32, 16)
-FIRST_MSG = (0, 2, 4, 8)
-N_MSG = 16
+CHAIN_ROWS = (16, 16, 16, 16)
+FIRST_MSG = tuple(sum(A_ROWS // size for size in CHAIN_ROWS[:i]) for i in range(len(CHAIN_ROWS)))
+N_MSG = sum(A_ROWS // size for size in CHAIN_ROWS)
 
 
 def kernel(rows, width, start_hbm, w_hbm, b_ref, s_ref, out_hbm,
@@ -40,8 +40,7 @@
     load_start = pltpu.make_async_copy(start_hbm, inbuf.at[0], start_sem)
     load_start.start()
     load_w = [pltpu.make_async_copy(w_hbm.at[l], w.at[l], w_sem.at[l]) for l in range(LAY_DEV)]
-    for c in load_w:
-        c.start()
+    load_w[0].start()
 
     barrier = pltpu.get_barrier_semaphore()
     peers = 0
@@ -207,7 +206,11 @@
 
     load_start.wait()
     load_w[0].wait()
-    lag = jnp.where(group <= 2, 1, jnp.where(group <= 5, 2, jnp.where(group <= 8, 3, 4)))
+    load_w[1].start()
+    late_finish = group < groups // 2
+    odd = lax.rem(p, 2)
+    lag = jnp.where(group <= 1, 1 - odd, jnp.where(
+        group <= 2, 1, jnp.where(group <= 5, 2, jnp.where(group <= 8, 3, 4))))
 
     def wave(step, _):
         def one_pass(k, _):
@@ -225,10 +228,20 @@
             @pl.when(group >= 1)
             def _():
                 chain(cb)
-            finish(cb)
+
+            @pl.when(jnp.logical_not(late_finish))
+            def _():
+                finish(cb)
         return 0
 
     lax.fori_loop(0, n_blocks + 6, wave, 0)
+
+    @pl.when(late_finish)
+    def _():
+        def one_finish(b, _):
+            finish(b)
+            return 0
+        lax.fori_loop(0, n_blocks, one_finish, 0)
 
     def drain(b, _):
         for l in range(LAY_DEV):

time: 168 us -> 144 us (0.86)
  Pallas kernels: 164 us -> 140 us
    pallas_call x1, Pallas kernels: 164 us -> 140 us  [local(): pl.pallas_call(functools.partial(kernel, rows, width), out_shape=jax.Shap...]
where the time goes in v2:
time: 144 us
  Pallas kernels  140 us (97%)
  local copies, waits for them, and re-layouts  3.76 us (3%)
    pallas_call x1, Pallas kernels, local(): pl.pallas_call(functools.partial(kernel, rows, width), out_shape=jax.Shap...  140 us
    unnamed x1, local copies, waits for them, and re-layouts  3.76 us

profile of v2, /device:TPU:102, one launch (start us, length us, event | category | flops | bytes accessed | tf_op | source)
XLA Modules:
  0.0 144.1 jit_solution(13702095460452279168)
XLA Ops:
  0.0 140.4 %shard_map.46 = bf16[2,512,1536]{2,1,0:T(8,128)(2,1)} custom-call(bf16[512,1536]{1,0:T(8,128)(2,1)} %bitcast.3, bf16[2,1536,1536]{2,1,0:T(8,128)(2,1)} %w_hbm.1, f32[2,1536]{1,0:T(2,128)} %b_ref.1, f32[2]{0:T(128)} %s_ref.1), custom_call_target="tpu_custom_call" | custom-call | tf_op jit(solution)/shard_map/pallas_call | solution.py:276
  140.4 3.8 %copy.6 = bf16[2,2,256,1536]{3,2,1,0:T(8,128)(2,1)} copy(bf16[2,2,256,1536]{3,2,1,0:T(8,128)(2,1)} %bitcast.2) | data formatting | bytes 6291456

commit v3 on v2

--- a/solution.py
+++ b/solution.py
@@ -13,11 +13,12 @@
 BF16 = jnp.bfloat16
 
 A_ROWS = 128
-N_CHUNK = 1
 PASS_COLS = 256
-CHAIN_ROWS = (16, 16, 16, 16)
-FIRST_MSG = tuple(sum(A_ROWS // size for size in CHAIN_ROWS[:i]) for i in range(len(CHAIN_ROWS)))
-N_MSG = sum(A_ROWS // size for size in CHAIN_ROWS)
+MSG_ROWS = 16
+PER_BLOCK = A_ROWS // MSG_ROWS
+EARLY_ROWS = (32, 32, 32, 32)
+LATE_ROWS = (16, 16, 16, 16)
+EARLY_GROUPS = 2
 
 
 def kernel(rows, width, start_hbm, w_hbm, b_ref, s_ref, out_hbm,
@@ -35,7 +36,6 @@
     res_back = (p + 1 >= 2 * INTERVAL) & has_next
     res_target = jnp.where(res_direct, p + 1, p + 1 - INTERVAL)
     res_slot = jnp.where(res_direct, 0, 1)
-    chunk = width // N_CHUNK
 
     load_start = pltpu.make_async_copy(start_hbm, inbuf.at[0], start_sem)
     load_start.start()
@@ -68,41 +68,32 @@
             send_sem=x_send.at[k, b], recv_sem=x_recv.at[k, b],
             device_id=(p + 1,), device_id_type=MESH)
 
-    def res_copy(m, r, size):
-        r = pl.multiple_of(r, size)
+    def res_copy(m):
+        r = pl.ds(pl.multiple_of(m * MSG_ROWS, MSG_ROWS), MSG_ROWS)
         return pltpu.make_async_remote_copy(
-            src_ref=xout.at[2, pl.ds(r, size)], dst_ref=inbox.at[res_slot, pl.ds(r, size)],
+            src_ref=xout.at[2, r], dst_ref=inbox.at[res_slot, r],
             send_sem=r_send.at[m], recv_sem=r_recv.at[res_slot, m],
             device_id=(res_target,), device_id_type=MESH)
 
-    def res_wait(slot, m, r, size):
-        r = pl.multiple_of(r, size)
+    def res_wait(slot, m):
+        r = pl.ds(pl.multiple_of(m * MSG_ROWS, MSG_ROWS), MSG_ROWS)
         pltpu.make_async_remote_copy(
-            src_ref=xout.at[2, pl.ds(r, size)], dst_ref=inbox.at[slot, pl.ds(r, size)],
+            src_ref=xout.at[2, r], dst_ref=inbox.at[slot, r],
             send_sem=r_send.at[m], recv_sem=r_recv.at[slot, m],
             device_id=(res_target,), device_id_type=MESH).wait_recv()
 
-    def msg_copy(m, r, size, c):
-        r = pl.multiple_of(r, size)
-        cols = slice(c * chunk, (c + 1) * chunk)
+    def msg_copy(m):
+        r = pl.ds(pl.multiple_of(m * MSG_ROWS, MSG_ROWS), MSG_ROWS)
         return pltpu.make_async_remote_copy(
-            src_ref=msgout.at[pl.ds(r, size), cols], dst_ref=inbox.at[0, pl.ds(r, size), cols],
-            send_sem=m_send.at[m, c], recv_sem=m_recv.at[m, c],
+            src_ref=msgout.at[r], dst_ref=inbox.at[0, r],
+            send_sem=m_send.at[m], recv_sem=m_recv.at[m],
             device_id=(p + INTERVAL,), device_id_type=MESH)
 
-    def messages(b, body):
-        for i, size in enumerate(CHAIN_ROWS):
-            if i and CHAIN_ROWS[i - 1] == size:
-                continue
-            same = [j for j in range(len(CHAIN_ROWS)) if CHAIN_ROWS[j] == size]
-            per = A_ROWS // size
-
-            @pl.when((b >= same[0]) & (b <= same[-1]))
-            def _():
-                def one(j, _):
-                    body(FIRST_MSG[same[0]] + (b - same[0]) * per + j, b * A_ROWS + j * size, size)
-                    return 0
-                lax.fori_loop(0, per, one, 0)
+    def messages(first, number, body):
+        def one(j, _):
+            body(first + j)
+            return 0
+        lax.fori_loop(0, number, one, 0)
 
     def relax(k, b, first):
         source = jnp.where(is_first, 0, k)
@@ -145,41 +136,60 @@
                 xout[2, r, :] = (xout[2, r, :].astype(F32) - xout[1, r, :].astype(F32)).astype(BF16)
                 return 0
             lax.fori_loop(0, A_ROWS // 16, diff, 0)
-            messages(b, lambda m, r, size: res_copy(m, r, size).start())
+            messages(b * PER_BLOCK, PER_BLOCK, lambda m: res_copy(m).start())
 
     def chain(b):
         coarse = (INTERVAL * LAY_DEV) * s_ref[0]
         anchor = jnp.where(is_first, 0, 2)
 
-        def one(m, r0, size):
-            r = pl.ds(pl.multiple_of(r0, size), size)
+        def one(r0, size):
+            r0 = pl.multiple_of(r0, size)
+            r = pl.ds(r0, size)
+            number = size // MSG_ROWS
+            m = r0 // MSG_ROWS
 
             @pl.when(group == 1)
             def _():
-                res_wait(0, m, r0, size)
+                messages(m, number, lambda i: res_wait(0, i))
 
             @pl.when(group > 1)
             def _():
-                for c in range(N_CHUNK):
-                    msg_copy(m, r0, size, c).wait_recv()
+                messages(m, number, lambda i: msg_copy(i).wait_recv())
 
             @pl.when(sends_msg)
             def _():
-                res_wait(1, m, r0, size)
+                messages(m, number, lambda i: res_wait(1, i))
             corr = inbox[0, r, :].astype(F32)
             x = (inbuf[anchor, r, :].astype(F32) + corr).astype(BF16)
-            for c in range(N_CHUNK):
-                cols = slice(c * chunk, (c + 1) * chunk)
-                pre = jnp.dot(x, w[0, :, cols], preferred_element_type=F32) + b_ref[0:1, cols]
-                t = jnp.tanh(pre)
-                d = inbox[0, r, cols].astype(F32) + coarse * (t - tbuf[r, cols])
-                msgout[r, cols] = (d + inbox[1, r, cols].astype(F32)).astype(BF16)
-                tbuf[r, cols] = t
-
-                @pl.when(sends_msg)
-                def _():
-                    msg_copy(m, r0, size, c).start()
-        messages(b, one)
+            if size > MSG_ROWS:
+                x = jnp.concatenate([x] * (A_ROWS // size), axis=0)
+            pre = jnp.dot(x, w[0], preferred_element_type=F32)[:size] + b_ref[0:1, :]
+            t = jnp.tanh(pre)
+            d = corr + coarse * (t - tbuf[r, :])
+            msgout[r, :] = (d + inbox[1, r, :].astype(F32)).astype(BF16)
+            tbuf[r, :] = t
+
+            @pl.when(sends_msg)
+            def _():
+                messages(m, number, lambda i: msg_copy(i).start())
+
+        early = group <= EARLY_GROUPS
+        for size in (64, 32, 16):
+            chosen = False
+            for i in range(rows // A_ROWS):
+                if EARLY_ROWS[i] == size:
+                    chosen = chosen | (early & (b == i))
+                if LATE_ROWS[i] == size:
+                    chosen = chosen | (jnp.logical_not(early) & (b == i))
+            if chosen is False:
+                continue
+
+            @pl.when(chosen)
+            def _():
+                def each(j, _):
+                    one(b * A_ROWS + j * size, size)
+                    return 0
+                lax.fori_loop(0, A_ROWS // size, each, 0)
 
     def out_copy(l, b):
         r = pl.ds(pl.multiple_of(b * A_ROWS, A_ROWS), A_ROWS)
@@ -254,14 +264,11 @@
 
         @pl.when(res_direct | res_back)
         def _():
-            messages(b, lambda m, r, size: res_copy(m, r, size).wait_send())
+            messages(b * PER_BLOCK, PER_BLOCK, lambda m: res_copy(m).wait_send())
 
         @pl.when(sends_msg)
         def _():
-            def sent(m, r, size):
-                for c in range(N_CHUNK):
-                    msg_copy(m, r, size, c).wait_send()
-            messages(b, sent)
+            messages(b * PER_BLOCK, PER_BLOCK, lambda m: msg_copy(m).wait_send())
         return 0
 
     lax.fori_loop(0, n_blocks, drain, 0)
@@ -272,6 +279,7 @@
     rows = initial.shape[0] * initial.shape[1]
     start = initial.reshape(rows, width)
     n_blocks = rows // A_ROWS
+    n_msg = rows // MSG_ROWS
     dma = pltpu.SemaphoreType.DMA
     states = pl.pallas_call(
         functools.partial(kernel, rows, width),
@@ -298,10 +306,10 @@
             dma((LAY_DEV, n_blocks)),
             dma((2, n_blocks)),
             dma((2, n_blocks)),
-            dma((N_MSG,)),
-            dma((2, N_MSG)),
-            dma((N_MSG, N_CHUNK)),
-            dma((N_MSG, N_CHUNK)),
+            dma((n_msg,)),
+            dma((2, n_msg)),
+            dma((n_msg,)),
+            dma((n_msg,)),
         ],
         compiler_params=pltpu.CompilerParams(
             collective_id=0, has_side_effects=True, vmem_limit_bytes=56 * 1024 * 1024),

time: 144 us -> 144 us (level)
  no operation moved by 1% of the time
where the time goes in v3:
time: 144 us
  Pallas kernels  140 us (97%)
  local copies, waits for them, and re-layouts  3.76 us (3%)
    pallas_call x1, Pallas kernels, local(): pl.pallas_call(functools.partial(kernel, rows, width), out_shape=jax.Shap...  140 us
    unnamed x1, local copies, waits for them, and re-layouts  3.76 us

profile of v3, /device:TPU:102, one launch (start us, length us, event | category | flops | bytes accessed | tf_op | source)
XLA Modules:
  0.0 143.6 jit_solution(6939183488640270493)
XLA Ops:
  0.0 139.8 %shard_map.46 = bf16[2,512,1536]{2,1,0:T(8,128)(2,1)} custom-call(bf16[512,1536]{1,0:T(8,128)(2,1)} %bitcast.3, bf16[2,1536,1536]{2,1,0:T(8,128)(2,1)} %w_hbm.1, f32[2,1536]{1,0:T(2,128)} %b_ref.1, f32[2]{0:T(128)} %s_ref.1), custom_call_target="tpu_custom_call" | custom-call | tf_op jit(solution)/shard_map/pallas_call | solution.py:284
  139.8 3.8 %copy.6 = bf16[2,2,256,1536]{3,2,1,0:T(8,128)(2,1)} copy(bf16[2,2,256,1536]{3,2,1,0:T(8,128)(2,1)} %bitcast.2) | data formatting | bytes 6291456

commit v4 on v3

--- a/solution.py
+++ b/solution.py
@@ -217,7 +217,7 @@
     load_start.wait()
     load_w[0].wait()
     load_w[1].start()
-    late_finish = group < groups // 2
+    late_finish = group < groups - 1
     odd = lax.rem(p, 2)
     lag = jnp.where(group <= 1, 1 - odd, jnp.where(
         group <= 2, 1, jnp.where(group <= 5, 2, jnp.where(group <= 8, 3, 4))))

time: 144 us -> 143 us (level)
  no operation moved by 1% of the time
where the time goes in v4:
time: 143 us
  Pallas kernels  139 us (97%)
  local copies, waits for them, and re-layouts  3.76 us (3%)
    pallas_call x1, Pallas kernels, local(): pl.pallas_call(functools.partial(kernel, rows, width), out_shape=jax.Shap...  139 us
    unnamed x1, local copies, waits for them, and re-layouts  3.76 us

profile of v4, /device:TPU:102, one launch (start us, length us, event | category | flops | bytes accessed | tf_op | source)
XLA Modules:
  0.0 143.1 jit_solution(18365293481556638562)
XLA Ops:
  0.0 139.3 %shard_map.46 = bf16[2,512,1536]{2,1,0:T(8,128)(2,1)} custom-call(bf16[512,1536]{1,0:T(8,128)(2,1)} %bitcast.3, bf16[2,1536,1536]{2,1,0:T(8,128)(2,1)} %w_hbm.1, f32[2,1536]{1,0:T(2,128)} %b_ref.1, f32[2]{0:T(128)} %s_ref.1), custom_call_target="tpu_custom_call" | custom-call | tf_op jit(solution)/shard_map/pallas_call | solution.py:284
  139.3 3.8 %copy.6 = bf16[2,2,256,1536]{3,2,1,0:T(8,128)(2,1)} copy(bf16[2,2,256,1536]{3,2,1,0:T(8,128)(2,1)} %bitcast.2) | data formatting | bytes 6291456
